TPU v7x, 32 devices: a whole 2x2x4 slice. The times are simulated.
32 devices in a mesh: wide: 8 (over y, x, core), narrow: 4 (over z).
Axes of the slice: x: 2, y: 2, z: 4, core: 2. Of those that a mesh axis runs over, the one named last changes fastest.
Arguments:
- states: bfloat16 [16384, 1024], P(('wide', 'narrow')), may hold values from -6 to 6
- applied: bfloat16 [16384, 1024], P(('wide', 'narrow')), may hold values from -6 to 6
- rotation: bfloat16 [2, 1024, 256], P(None, 'wide', 'narrow'), may hold values from -0.1875 to 0.1875
- ritz: float32 [2, 256], replicated, may hold values from 0.5 to 4
- potential: float32 [16384], P(('wide', 'narrow')), may hold values from 0.5 to 8
Outputs:
- rotated: bfloat16 [16384, 2, 256], P(('wide', 'narrow'))
- correction: bfloat16 [16384, 2, 256], P(('wide', 'narrow'))
- margin: float32 [2, 1024, 256], P(None, 'wide', 'narrow')
All inputs are finite; a program needn't handle non-finite values.
Results may differ from a plain program's by a relative error of at most 0.0095.
Values may be sent and summed in bfloat16 or wider, within the bound.
A program may use at most 64 MiB of HBM per device.

v0:
```python
import math
import jax
import jax.numpy as jnp
from jax import lax
from jax.sharding import PartitionSpec as P


def per_device(states, applied, rotation, ritz, potential):
    row_count = states.shape[0]
    total_rows = row_count * lax.axis_size("wide") * lax.axis_size("narrow")
    factor = 1.0 / math.sqrt(total_rows)
    contract = (((0,), (0,)), ((), ()))
    rotated_list = []
    correction_list = []
    margin_list = []
    for window in range(rotation.shape[0]):
        q_local = rotation[window]
        q_tall = lax.all_gather(q_local, "wide", axis=0, tiled=True)
        q_full = lax.all_gather(q_tall, "narrow", axis=1, tiled=True)
        plain = jnp.dot(states, q_full, preferred_element_type=jnp.float32)
        mapped = jnp.dot(applied, q_full, preferred_element_type=jnp.float32)
        eigen_values = ritz[window]
        residual = mapped - plain * eigen_values[None, :]
        fixed = (residual / (potential[:, None] + eigen_values[None, :])).astype(jnp.bfloat16)
        partial_value = lax.psum_scatter(
            lax.dot_general(states, fixed, contract, preferred_element_type=jnp.float32).astype(
                jnp.bfloat16
            ),
            "wide",
            scatter_dimension=0,
            tiled=True,
        )
        summed = lax.psum_scatter(partial_value, "narrow", scatter_dimension=1, tiled=True).astype(
            jnp.float32
        )
        rotated_list.append(plain.astype(jnp.bfloat16))
        correction_list.append(fixed)
        margin_list.append(summed * factor)
    return (
        jnp.stack(rotated_list, axis=1),
        jnp.stack(correction_list, axis=1),
        jnp.stack(margin_list, axis=0),
    )


def solution(mesh):
    placed = (
        P(("wide", "narrow"), None),
        P(("wide", "narrow"), None),
        P(None, "wide", "narrow"),
        P(),
        P(("wide", "narrow")),
    )
    return jax.shard_map(
        per_device,
        mesh=mesh,
        in_specs=placed,
        out_specs=(
            P(("wide", "narrow"), None, None),
            P(("wide", "narrow"), None, None),
            P(None, "wide", "narrow"),
        ),
        check_vma=False,
    )
```

profile of v0, /device:TPU:0, one launch (start us, length us, event | category | flops | bytes accessed | tf_op | source)
XLA Modules:
  0.0 160.5 jit_solution(8119105058409660867)
XLA Ops:
  7.2 0.8 fusion.13
  8.0 0.7 fusion.12
  8.7 10.5 %all-gather.2 = bf16[1,1024,64]{1,2,0:T(8,128)(2,1)S(1)} all-gather(bf16[1,128,64]{1,2,0:T(8,128)(2,1)S(1)} %get-tuple-element.10), channel_id=4, replica_groups=mesh['wide'=8,'narrow'=4] {'wide'}, dimensions={1}, use_global_device_ids=true | all-gather | bytes 147456 | tf_op jit(solution)/shard_map/all_gather | solution.py:18
  19.3 16.3 %all-gather.3 = bf16[1,1024,256]{1,2,0:T(8,128)(2,1)S(1)} all-gather(bf16[1,1024,64]{1,2,0:T(8,128)(2,1)S(1)} %all-gather.2), channel_id=5, replica_groups=mesh['wide'=8,'narrow'=4] {'narrow'}, dimensions={2}, use_global_device_ids=true | all-gather | bytes 655360 | tf_op jit(solution)/shard_map/all_gather | solution.py:19
  35.6 0.5 fusion.7
  36.1 0.7 copy-done.1
  36.8 0.5 fusion.4
  37.3 0.5 fusion.3
  37.8 1.0 copy.14
  38.8 0.0 reduce-scatter.13.cloned.1.call-start
  38.9 9.0 %all-gather = bf16[1,1024,64]{1,2,0:T(8,128)(2,1)S(1)} all-gather(bf16[1,128,64]{1,2,0:T(8,128)(2,1)S(1)} %get-tuple-element.9), channel_id=2, replica_groups=mesh['wide'=8,'narrow'=4] {'wide'}, dimensions={1}, use_global_device_ids=true | all-gather | bytes 147456 | tf_op jit(solution)/shard_map/all_gather | solution.py:18
  47.9 16.6 %all-gather.1 = bf16[1,1024,256]{1,2,0:T(8,128)(2,1)S(1)} all-gather(bf16[1,1024,64]{1,2,0:T(8,128)(2,1)S(1)} %all-gather), channel_id=3, replica_groups=mesh['wide'=8,'narrow'=4] {'narrow'}, dimensions={2}, use_global_device_ids=true | all-gather | bytes 655360 | tf_op jit(solution)/shard_map/all_gather | solution.py:19
  64.5 0.5 fusion.10
  65.0 0.7 copy-done.2
  65.7 0.5 fusion.5
  66.2 0.5 fusion.2
  66.6 1.0 copy.12
  67.7 0.0 reduce-scatter.11.cloned.1.call-start
  67.8 5.8 %reduce-scatter.15.cloned.1.call-done = bf16[128,256]{1,0:T(8,128)(2,1)} async-done(((bf16[1024,256]{1,0:T(8,128)(2,1)}), bf16[128,256]{1,0:T(8,128)(2,1)}) %reduce-scatter.15.cloned.1.call-update) | async-done | bytes 65552
  73.6 1.6 copy.15
  75.2 0.0 reduce-scatter.9.cloned.1.call-start
  75.3 0.1 pad_maximum_fusion
  75.3 1.3 copy.10
  76.7 0.1 pad_maximum_fusion.1
  76.7 1.3 copy.11
  78.0 32.8 %reduce-scatter.13.cloned.1.call-done = bf16[128,256]{1,0:T(8,128)(2,1)} async-done(((bf16[1024,256]{1,0:T(8,128)(2,1)}), bf16[128,256]{1,0:T(8,128)(2,1)}) %reduce-scatter.13.cloned.1.call-update) | async-done | bytes 65552
  110.9 1.6 copy.13
  112.5 20.6 %reduce-scatter.11.cloned.1.call-done = bf16[128,64]{0,1:T(8,128)(2,1)} async-done(((bf16[128,256]{0,1:T(8,128)(2,1)}), bf16[128,64]{0,1:T(8,128)(2,1)}) %reduce-scatter.11.cloned.1.call-update) | async-done | bytes 16400 | tf_op jit(solution)/shard_map/reduce_scatter | solution.py:33
  133.0 0.7 multiply_bitcast_fusion
  133.7 18.9 %reduce-scatter.9.cloned.1.call-done = bf16[128,64]{0,1:T(8,128)(2,1)} async-done(((bf16[128,256]{0,1:T(8,128)(2,1)}), bf16[128,64]{0,1:T(8,128)(2,1)}) %reduce-scatter.9.cloned.1.call-update) | async-done | bytes 16400 | tf_op jit(solution)/shard_map/reduce_scatter | solution.py:33
  152.6 0.7 multiply_bitcast_fusion.1
  153.3 0.6 pad_maximum_fusion.2
  (13 shorter events, 0.2 us)
Async XLA Ops:
  7.2 28.4 %copy-start = (bf16[512,1024]{1,0:T(8,128)(2,1)S(1)}, bf16[512,1024]{1,0:T(8,128)(2,1)}, u32[]{:S(2)}) copy-start(bf16[512,1024]{1,0:T(8,128)(2,1)} %param.5) | copy-start | bytes 3145732
  7.2 66.4 %reduce-scatter.15.cloned.1.call-start = ((), (), s32[]{:S(2)}) async-start(), calls=%async_computation.7 | async-start | bytes 589824
  35.6 1.2 copy-start.1
  36.1 0.7 copy-start.3
  38.8 72.1 %reduce-scatter.13.cloned.1.call-start = ((), (), s32[]{:S(2)}) async-start(), calls=%async_computation.6 | async-start | bytes 589824
  64.5 1.2 copy-start.2
  67.7 65.3 %reduce-scatter.11.cloned.1.call-start = ((), (), s32[]{:S(2)}) async-start(), calls=%async_computation.5 | async-start | bytes 81920 | tf_op jit(solution)/shard_map/reduce_scatter | solution.py:33
  75.2 77.4 %reduce-scatter.9.cloned.1.call-start = ((), (), s32[]{:S(2)}) async-start(), calls=%async_computation.4 | async-start | bytes 81920 | tf_op jit(solution)/shard_map/reduce_scatter | solution.py:33
Sparse Core Ops, SparseCore 0:
  38.9 34.6 reduce-scatter.14
  76.7 34.1 reduce-scatter.12
  113.7 19.2 reduce-scatter.10
  135.1 17.4 reduce-scatter.8
where the time goes:
time: 161 us; the launch traced here: 160 us
  waiting for transfers between devices  78.1 us (49%)
  blocking collectives  52.5 us (33%)
  between operations  13.9 us (9%)
  local copies, waits for them, and re-layouts  10.8 us (7%)
  matrix products  2.82 us (2%)
  other arithmetic  2.24 us (1%)
    reduce_scatter x2, waiting for transfers between devices, per_device(): lax.psum_scatter(partial_value, 'narrow', scatter_dimension=1, tiled=True)  39.4 us
    unnamed x6, waiting for transfers between devices  38.7 us
    all_gather x2, blocking collectives, per_device(): q_full = lax.all_gather(q_tall, 'narrow', axis=1, tiled=True)  32.9 us
    all_gather x2, blocking collectives, per_device(): q_tall = lax.all_gather(q_local, 'wide', axis=0, tiled=True)  19.6 us
    unnamed x14, local copies, waits for them, and re-layouts  9.3 us
  transfers between devices with their start and end apart: 4, of which 4 were waited for; matrix products, arithmetic and copies ran while one was open for 6% of the time, Pallas kernels for 0%

commit v1 on v0

--- a/solution.py
+++ b/solution.py
@@ -3,6 +3,18 @@
 import jax.numpy as jnp
 from jax import lax
 from jax.sharding import PartitionSpec as P
+
+
+def doubled_up(array, axis, dim):
+    ways, here, lap = (lax.axis_size(axis), lax.axis_index(axis), array.shape[dim])
+    line, have = (array, 1)
+    while have < ways:
+        line = jnp.concatenate(
+            [line, lax.ppermute(line, axis, [(d, (d - have) % ways) for d in range(ways)])],
+            axis=dim,
+        )
+        have = 2 * have
+    return jnp.roll(line, here * lap, axis=dim)
 
 
 def per_device(states, applied, rotation, ritz, potential):
@@ -16,7 +28,7 @@
     for window in range(rotation.shape[0]):
         q_local = rotation[window]
         q_tall = lax.all_gather(q_local, "wide", axis=0, tiled=True)
-        q_full = lax.all_gather(q_tall, "narrow", axis=1, tiled=True)
+        q_full = doubled_up(q_tall, "narrow", 1)
         plain = jnp.dot(states, q_full, preferred_element_type=jnp.float32)
         mapped = jnp.dot(applied, q_full, preferred_element_type=jnp.float32)
         eigen_values = ritz[window]

time: 161 us -> 185 us (1.15)
  waiting for transfers between devices: 78.1 us -> 129 us
  blocking collectives: 52.5 us -> 19.5 us
  starting transfers between devices: 0.16 us -> 4.36 us
  other arithmetic: 2.24 us -> 4.3 us
    all_gather x2 -> x0, blocking collectives: 32.9 us -> none  [per_device(): q_full = lax.all_gather(q_tall, 'narrow', axis=1, tiled=True)]
    unnamed x6, waiting for transfers between devices: 38.7 us -> 64 us
    ppermute x0 -> x4, waiting for transfers between devices: none -> 25.3 us  [doubled_up(): lax.ppermute(line, axis, [(d, (d - have) % ways) for d in range(ways)])]
    ppermute x0 -> x4, starting transfers between devices: none -> 4.19 us  [doubled_up(): lax.ppermute(line, axis, [(d, (d - have) % ways) for d in range(ways)])]
    concatenate x0 -> x3, other arithmetic: none -> 2.05 us  [the longest x1 2.02 us: doubled_up(): return jnp.roll(line, here * lap, axis=dim)]
    unnamed x14 -> x20, local copies, waits for them, and re-layouts: 9.3 us -> 10.2 us
  transfers between devices with their start and end apart: 4 -> 8, of which waited for: 4 -> 7; matrix products, arithmetic and copies ran while one was open for 6% -> 5% of each run, Pallas kernels for 0% -> 0%
where the time goes in v1:
time: 185 us
  waiting for transfers between devices  129 us (70%)
  blocking collectives  19.5 us (11%)
  between operations  14 us (8%)
  local copies, waits for them, and re-layouts  11 us (6%)
  starting transfers between devices  4.36 us (2%)
  other arithmetic  4.3 us (2%)
  matrix products  2.8 us (2%)
    unnamed x6, waiting for transfers between devices  64 us
    reduce_scatter x2, waiting for transfers between devices, per_device(): lax.psum_scatter(partial_value, 'narrow', scatter_dimension=1, tiled=True)  39.4 us
    ppermute x4, waiting for transfers between devices, doubled_up(): lax.ppermute(line, axis, [(d, (d - have) % ways) for d in range(ways)])  25.3 us
    all_gather x2, blocking collectives, per_device(): q_tall = lax.all_gather(q_local, 'wide', axis=0, tiled=True)  19.5 us
    unnamed x20, local copies, waits for them, and re-layouts  10.2 us
    ppermute x4, starting transfers between devices, doubled_up(): lax.ppermute(line, axis, [(d, (d - have) % ways) for d in range(ways)])  4.19 us
  transfers between devices with their start and end apart: 8, of which 7 were waited for; matrix products, arithmetic and copies ran while one was open for 5% of the time, Pallas kernels for 0%

profile of v1, /device:TPU:0, one launch (start us, length us, event | category | flops | bytes accessed | tf_op | source)
XLA Modules:
  0.0 184.7 jit_solution(4152002219181986047)
XLA Ops:
  7.2 0.8 fusion.18
  8.0 10.5 %all-gather.1 = bf16[1,1024,64]{1,2,0:T(8,128)(2,1)S(1)} all-gather(bf16[1,128,64]{1,2,0:T(8,128)(2,1)S(1)} %get-tuple-element.11), channel_id=3, replica_groups=mesh['wide'=8,'narrow'=4] {'wide'}, dimensions={1}, use_global_device_ids=true | all-gather | bytes 147456 | tf_op jit(solution)/shard_map/all_gather | solution.py:30
  18.6 3.6 %collective-permute-start.2 = (bf16[1024,64]{0,1:T(8,128)(2,1)S(1)}, bf16[1024,64]{0,1:T(8,128)(2,1)S(1)}, u32[]{:S(2)}, u32[]{:S(2)}) collective-permute-start(bf16[1024,64]{0,1:T(8,128)(2,1)S(1)} %bitcast.48), channel_id=1, source_target_pairs={{0,3},{1,0},{2,1},{3,2},{4,7},{5,4},{6,5},{7,6},{8,11},{9,8},{10,9... | collective-permute-start | bytes 393224 | tf_op jit(solution)/shard_map/ppermute | solution.py:13
  22.2 9.0 %all-gather = bf16[1,1024,64]{1,2,0:T(8,128)(2,1)S(1)} all-gather(bf16[1,128,64]{1,2,0:T(8,128)(2,1)S(1)} %get-tuple-element.10), channel_id=2, replica_groups=mesh['wide'=8,'narrow'=4] {'wide'}, dimensions={1}, use_global_device_ids=true | all-gather | bytes 147456 | tf_op jit(solution)/shard_map/all_gather | solution.py:30
  31.2 0.4 collective-permute-start
  31.7 6.3 %collective-permute-done = bf16[1024,64]{0,1:T(8,128)(2,1)S(1)} collective-permute-done((bf16[1024,64]{0,1:T(8,128)(2,1)S(1)}, bf16[1024,64]{0,1:T(8,128)(2,1)S(1)}, u32[]{:S(2)}, u32[]{:S(2)}) %collective-permute-start) | collective-permute-done | bytes 131104 | tf_op jit(solution)/shard_map/ppermute | solution.py:13
  38.1 0.7 copy-done.3
  38.8 14.3 %collective-permute-done.3 = bf16[1024,128]{0,1:T(8,128)(2,1)S(1)} collective-permute-done((bf16[1024,128]{0,1:T(8,128)(2,1)S(1)}, bf16[1024,128]{0,1:T(8,128)(2,1)S(1)}, u32[]{:S(2)}, u32[]{:S(2)}) %collective-permute-start.3) | collective-permute-done | bytes 262176 | tf_op jit(solution)/shard_map/ppermute | solution.py:13
  53.1 4.7 %collective-permute-done.1 = bf16[1024,128]{0,1:T(8,128)(2,1)S(1)} collective-permute-done((bf16[1024,128]{0,1:T(8,128)(2,1)S(1)}, bf16[1024,128]{0,1:T(8,128)(2,1)S(1)}, u32[]{:S(2)}, u32[]{:S(2)}) %collective-permute-start.1) | collective-permute-done | bytes 262176 | tf_op jit(solution)/shard_map/ppermute | solution.py:13
  57.8 2.0 %fusion.10 = (bf16[1024,256]{0,1:T(8,128)(2,1)S(1)}, bf16[1024,256]{0,1:T(8,128)(2,1)S(1)}) fusion(s32[]{:T(128)S(6)} %select_n.13, bf16[1024,64]{0,1:T(8,128)(2,1)S(1)} %bitcast.50, bf16[1024,64]{0,1:T(8,128)(2,1)S(1)} %collective-permute-done.2, bf16[1024,128]{0,1:T(8,128)(2,1)S(1)} %collective-permute-done.3, ...), kind=kLoop, calls=%fused_computation.26 | loop fusion | flops 6291456 | bytes 2097156 | tf_op jit(solution)/shard_map/jit(_roll_dynamic)/concatenate | solution.py:17
  59.9 0.5 fusion.20
  60.4 0.7 copy-done.4
  61.1 0.5 fusion.7
  61.6 0.4 fusion.4
  62.0 1.0 copy.12
  63.1 0.5 fusion.21
  63.6 0.7 copy-done.5
  64.3 0.5 fusion.6
  64.8 0.7 copy-done.1
  65.5 0.4 fusion.5
  66.0 1.0 copy.14
  67.1 30.7 %reduce-scatter.13.cloned.1.call-done = bf16[128,256]{1,0:T(8,128)(2,1)} async-done(((bf16[1024,256]{1,0:T(8,128)(2,1)}), bf16[128,256]{1,0:T(8,128)(2,1)}) %reduce-scatter.13.cloned.1.call-update) | async-done | bytes 65552
  97.8 1.6 copy.13
  99.6 1.1 copy.10
  100.7 1.1 copy.11
  101.8 33.3 %reduce-scatter.15.cloned.1.call-done = bf16[128,256]{1,0:T(8,128)(2,1)} async-done(((bf16[1024,256]{1,0:T(8,128)(2,1)}), bf16[128,256]{1,0:T(8,128)(2,1)}) %reduce-scatter.15.cloned.1.call-update) | async-done | bytes 65552
  135.1 1.6 copy.15
  136.7 20.0 %reduce-scatter.9.cloned.1.call-done = bf16[128,64]{0,1:T(8,128)(2,1)} async-done(((bf16[128,256]{0,1:T(8,128)(2,1)}), bf16[128,64]{0,1:T(8,128)(2,1)}) %reduce-scatter.9.cloned.1.call-update) | async-done | bytes 16400 | tf_op jit(solution)/shard_map/reduce_scatter | solution.py:45
  156.7 0.7 multiply_bitcast_fusion.1
  157.4 19.5 %reduce-scatter.11.cloned.1.call-done = bf16[128,64]{0,1:T(8,128)(2,1)} async-done(((bf16[128,256]{0,1:T(8,128)(2,1)}), bf16[128,64]{0,1:T(8,128)(2,1)}) %reduce-scatter.11.cloned.1.call-update) | async-done | bytes 16400 | tf_op jit(solution)/shard_map/reduce_scatter | solution.py:45
  176.8 0.7 multiply_bitcast_fusion
  177.6 0.6 pad_maximum_fusion.4
  (28 shorter events, 0.6 us)
Async XLA Ops:
  7.2 52.7 %copy-start = (bf16[512,1024]{1,0:T(8,128)(2,1)S(1)}, bf16[512,1024]{1,0:T(8,128)(2,1)}, u32[]{:S(2)}) copy-start(bf16[512,1024]{1,0:T(8,128)(2,1)} %param.7) | copy-start | bytes 3145732
  7.2 90.7 %reduce-scatter.13.cloned.1.call-start = ((), (), s32[]{:S(2)}) async-start(), calls=%async_computation.6 | async-start | bytes 589824
  18.6 13.1 %collective-permute-start.2 = (bf16[1024,64]{0,1:T(8,128)(2,1)S(1)}, bf16[1024,64]{0,1:T(8,128)(2,1)S(1)}, u32[]{:S(2)}, u32[]{:S(2)}) collective-permute-start(bf16[1024,64]{0,1:T(8,128)(2,1)S(1)} %bitcast.48), channel_id=1, source_target_pairs={{0,3},{1,0},{2,1},{3,2},{4,7},{5,4},{6,5},{7,6},{8,11},{9,8},{10,9... | collective-permute-start | bytes 393224 | tf_op jit(solution)/shard_map/ppermute | solution.py:13
  31.2 6.8 %collective-permute-start = (bf16[1024,64]{0,1:T(8,128)(2,1)S(1)}, bf16[1024,64]{0,1:T(8,128)(2,1)S(1)}, u32[]{:S(2)}, u32[]{:S(2)}) collective-permute-start(bf16[1024,64]{0,1:T(8,128)(2,1)S(1)} %bitcast.51), channel_id=1, source_target_pairs={{0,3},{1,0},{2,1},{3,2},{4,7},{5,4},{6,5},{7,6},{8,11},{9,8},{10,9... | collective-permute-start | bytes 393224 | tf_op jit(solution)/shard_map/ppermute | solution.py:13
  31.7 21.4 %collective-permute-start.3 = (bf16[1024,128]{0,1:T(8,128)(2,1)S(1)}, bf16[1024,128]{0,1:T(8,128)(2,1)S(1)}, u32[]{:S(2)}, u32[]{:S(2)}) collective-permute-start(bf16[1024,128]{0,1:T(8,128)(2,1)S(1)} %pad_maximum_fusion.3), channel_id=1, source_target_pairs={{0,2},{1,3},{2,0},{3,1},{4,6},{5,7},{6,4},{7,5},{8,10},{9,11},{10,... | collective-permute-start | bytes 786440 | tf_op jit(solution)/shard_map/ppermute | solution.py:13
  38.0 19.8 %collective-permute-start.1 = (bf16[1024,128]{0,1:T(8,128)(2,1)S(1)}, bf16[1024,128]{0,1:T(8,128)(2,1)S(1)}, u32[]{:S(2)}, u32[]{:S(2)}) collective-permute-start(bf16[1024,128]{0,1:T(8,128)(2,1)S(1)} %pad_maximum_fusion.2), channel_id=1, source_target_pairs={{0,2},{1,3},{2,0},{3,1},{4,6},{5,7},{6,4},{7,5},{8,10},{9,11},{10,... | collective-permute-start | bytes 786440 | tf_op jit(solution)/shard_map/ppermute | solution.py:13
  38.1 0.7 copy-start.3
  59.8 1.2 copy-start.4
  60.3 0.7 copy-start.6
  63.1 72.0 %reduce-scatter.15.cloned.1.call-start = ((), (), s32[]{:S(2)}) async-start(), calls=%async_computation.7 | async-start | bytes 589824
  63.1 1.2 copy-start.5
  64.8 0.7 copy-start.1
  67.0 89.7 %reduce-scatter.9.cloned.1.call-start = ((), (), s32[]{:S(2)}) async-start(), calls=%async_computation.4 | async-start | bytes 81920 | tf_op jit(solution)/shard_map/reduce_scatter | solution.py:45
  99.4 77.4 %reduce-scatter.11.cloned.1.call-start = ((), (), s32[]{:S(2)}) async-start(), calls=%async_computation.5 | async-start | bytes 81920 | tf_op jit(solution)/shard_map/reduce_scatter | solution.py:45
  99.5 1.1 copy-start.2
Sparse Core Ops, SparseCore 0:
  63.2 34.6 reduce-scatter.12
  100.9 34.1 reduce-scatter.14
  137.3 19.2 reduce-scatter.8
  159.3 17.4 reduce-scatter.10
